TPU v7x, 32 devices: a whole 2x2x4 slice. The times are simulated.
32 devices in a mesh: dp: 16 (over z, x, core), tensor: 2 (over y).
Axes of the slice: x: 2, y: 2, z: 4, core: 2. Of those that a mesh axis runs over, the one named last changes fastest.
Arguments:
- tokens: bfloat16 [8192, 2048], P('dp'), may hold values from -6 to 6
- segments: int32 [16, 512], P('dp'), may hold values from 0 to 3, never falling along the last dimension, each value on 1 to 384 neighbouring positions
- cotangent: bfloat16 [8192, 2048], P('dp'), may hold values from -6 to 6
- norm_gain: float32 [2048], P('dp'), may hold values from 0.1 to 1.9
- attn_weight: float32 [2048, 4, 2048], P('dp', None, 'tensor'), may hold values from -0.125 to 0.125
- beta_weight: float32 [2048, 16], P('dp', 'tensor'), may hold values from -0.125 to 0.125
- conv_weight: float32 [3, 4, 16, 128], P(None, None, 'tensor', 'dp'), may hold values from -3 to 3
- out_gain: float32 [128], P('dp'), may hold values from 0.1 to 1.9
- mlp_gain: float32 [2048], P('dp'), may hold values from 0.1 to 1.9
- mlp_weight: float32 [2048, 3, 5632], P('dp', None, 'tensor'), may hold values from -0.125 to 0.125
Outputs:
- output: bfloat16 [8192, 2048], P('dp')
- input_grad: float32 [8192, 2048], P('dp')
- norm_gain_grad: float32 [2048], P('dp')
- attn_weight_grad: float32 [2048, 4, 2048], P('dp', None, 'tensor')
- beta_weight_grad: float32 [2048, 16], P('dp', 'tensor')
- conv_weight_grad: float32 [3, 4, 16, 128], P(None, None, 'tensor', 'dp')
- out_gain_grad: float32 [128], P('dp')
- mlp_gain_grad: float32 [2048], P('dp')
- mlp_weight_grad: float32 [2048, 3, 5632], P('dp', None, 'tensor')
Inputs may be any that keep to these rules, and one draw needn't show every extreme that they name: `segments`: within a sequence the numbers never fall; a document (a run of one number) has 1 to 384 tokens, and some document has exactly 384.
All inputs are finite; a program needn't handle non-finite values.
Results may differ from a plain program's by a relative error of at most 0.017.
The roundings to bfloat16 on the way count: a program that leaves them out, or rounds other values in their place, can miss the bound.
Values may be sent and summed in bfloat16 or wider, within the bound.
No kernel may reach another device: no remote copies, remote signals or barrier semaphores. Data moves between devices by JAX's collectives and lax.ppermute only.
A program may use at most 384 MiB of HBM per device.

v0:
```python
import jax
import jax.numpy as jnp
from jax import lax
from jax.sharding import PartitionSpec as P

BLOCK = 64
highest = lax.Precision.HIGHEST


def rms_scale(values, gain_values, epsilon):
    return (
        values
        * lax.rsqrt(jnp.mean(values * values, axis=-1, keepdims=True) + epsilon)
        * gain_values
    )


def norm_apply(values, gain_values):
    return rms_scale(values, gain_values, 1e-05)


def short_conv(signal, weight, seg_ids):
    length = signal.shape[0]
    summed = signal * weight[3]
    for offset in range(1, 4):
        pad_rows = jnp.zeros((offset,) + signal.shape[1:], signal.dtype)
        shifted = jnp.concatenate([pad_rows, signal[: length - offset]], axis=0)
        prior_ids = jnp.concatenate(
            [jnp.full((offset,), -1, jnp.int32), seg_ids[: length - offset]], axis=0
        )
        allowed = (prior_ids == seg_ids).astype(signal.dtype)
        summed = summed + shifted * allowed[:, None, None] * weight[3 - offset]
    return summed


def delta_block(memory, inputs):
    queries, key_vecs, values, strength, seg_ids, prior_id = inputs
    block_len = seg_ids.shape[0]
    carry_in = (seg_ids == prior_id).astype(queries.dtype)
    same_doc = (seg_ids[:, None] == seg_ids[None, :]).astype(queries.dtype)
    row_ids = jnp.arange(block_len)
    strict = (row_ids[:, None] > row_ids[None, :]).astype(queries.dtype)
    causal = (row_ids[:, None] >= row_ids[None, :]).astype(queries.dtype)
    key_inner = jnp.einsum("ihd,jhd->hij", key_vecs, key_vecs, precision=highest) * (
        same_doc * strict
    )
    weights_t = jnp.transpose(strength)
    system = jnp.eye(block_len, dtype=queries.dtype) + weights_t[:, :, None] * key_inner
    recalled = jnp.einsum("hvd,ihd->hiv", memory, key_vecs, precision=highest)
    target = weights_t[:, :, None] * (
        jnp.transpose(values, (1, 0, 2)) - carry_in[None, :, None] * recalled
    )
    writes = lax.linalg.triangular_solve(
        system, target, left_side=True, lower=True, unit_diagonal=True
    )
    scores = jnp.einsum("ihd,jhd->hij", queries, key_vecs, precision=highest) * (same_doc * causal)
    carried = jnp.einsum("hvd,ihd->hiv", memory, queries, precision=highest)
    output = carry_in[None, :, None] * carried + jnp.einsum(
        "hij,hjv->hiv", scores, writes, precision=highest
    )
    final_doc = same_doc[block_len - 1]
    updated = carry_in[block_len - 1] * memory + jnp.einsum(
        "hjv,jhd->hvd", writes * final_doc[None, :, None], key_vecs, precision=highest
    )
    return (updated, jnp.transpose(output, (1, 0, 2)))


def delta_sequence(queries, key_vecs, values, strength, seg_ids):
    length = queries.shape[0]
    head_count = queries.shape[1]
    head_width = queries.shape[2]
    block_count = length // BLOCK
    prior_ids = jnp.concatenate(
        [jnp.full((1,), -1, jnp.int32), seg_ids[BLOCK - 1 : length - 1 : BLOCK]], axis=0
    )

    def blocked(array_in):
        return array_in.reshape((block_count, BLOCK) + array_in.shape[1:])

    initial = jnp.zeros((head_count, head_width, head_width), queries.dtype)
    final_state, outputs = lax.scan(
        jax.checkpoint(delta_block),
        initial,
        (
            blocked(queries),
            blocked(key_vecs),
            blocked(values),
            blocked(strength),
            blocked(seg_ids),
            prior_ids,
        ),
    )
    return outputs.reshape(queries.shape)


def token_mixer(projected, beta_logits, conv_weight, out_gain, seg_ids):
    length = projected.shape[0]
    convolved = [
        jax.nn.silu(short_conv(projected[:, which], conv_weight[which], seg_ids))
        for which in range(3)
    ]
    queries = convolved[0] * lax.rsqrt(
        jnp.sum(convolved[0] * convolved[0], axis=-1, keepdims=True) + 1e-06
    )
    key_vecs = convolved[1] * lax.rsqrt(
        jnp.sum(convolved[1] * convolved[1], axis=-1, keepdims=True) + 1e-06
    )
    strength = jax.nn.sigmoid(beta_logits)
    output = delta_sequence(queries, key_vecs, convolved[2], strength, seg_ids)
    return rms_scale(output, out_gain, 1e-05).reshape(length, -1)


def body(
    tokens,
    segments,
    cotangent,
    norm_gain,
    attn_weight,
    beta_weight,
    conv_weight,
    out_gain,
    mlp_gain,
    mlp_weight,
):
    seg_ids = segments[0]
    length = tokens.shape[0]
    gain_in_low = norm_gain.astype(jnp.bfloat16)
    attn_low = attn_weight.astype(jnp.bfloat16)
    beta_low = beta_weight.astype(jnp.bfloat16)
    gain_mid_low = mlp_gain.astype(jnp.bfloat16)
    mlp_low = mlp_weight.astype(jnp.bfloat16)
    gain_in, attn_mat, beta_mat, conv_full, gain_heads = (
        lax.all_gather(gain_in_low, "dp", axis=0, tiled=True),
        lax.all_gather(attn_low, "dp", axis=0, tiled=True),
        lax.all_gather(beta_low, "dp", axis=0, tiled=True),
        lax.all_gather(conv_weight.astype(jnp.bfloat16), "dp", axis=3, tiled=True),
        lax.all_gather(out_gain.astype(jnp.bfloat16), "dp", axis=0, tiled=True),
    )
    gain_mid, mlp_mat = (
        lax.all_gather(gain_mid_low, "dp", axis=0, tiled=True),
        lax.all_gather(mlp_low, "dp", axis=0, tiled=True),
    )
    model_width = attn_mat.shape[0]
    local_width = attn_mat.shape[2]
    head_count = conv_full.shape[2]
    head_width = conv_full.shape[3]
    inputs_f = tokens.astype(jnp.float32)
    normed = rms_scale(inputs_f, gain_in.astype(jnp.float32), 1e-05).astype(jnp.bfloat16)
    qkv_mat = attn_mat[:, :3].reshape(model_width, 3 * local_width)
    projected = jnp.dot(normed, qkv_mat, preferred_element_type=jnp.float32)
    beta_logits = jnp.dot(normed, beta_mat, preferred_element_type=jnp.float32)

    def local_mixer(proj_value, logit_value, conv_value, heads_gain):
        return token_mixer(
            proj_value.reshape(length, 3, head_count, head_width),
            logit_value,
            conv_value,
            heads_gain,
            seg_ids,
        )

    mixed, mixer_pull = jax.vjp(
        local_mixer,
        projected,
        beta_logits,
        conv_full.astype(jnp.float32),
        gain_heads.astype(jnp.float32),
    )
    mixed_low = mixed.astype(jnp.bfloat16)
    attn_part = jnp.einsum(
        "tc,oc->to", mixed_low, attn_mat[:, 3], preferred_element_type=jnp.float32
    )
    attended = lax.psum(attn_part, "tensor")
    hidden = inputs_f + attended
    normed_mlp = rms_scale(hidden, gain_mid.astype(jnp.float32), 1e-05).astype(jnp.bfloat16)
    gate_up = jnp.einsum(
        "td,dgf->tgf", normed_mlp, mlp_mat[:, :2], preferred_element_type=jnp.float32
    )
    gate_vals = gate_up[:, 0]
    up_vals = gate_up[:, 1]
    activated = (jax.nn.silu(gate_vals) * up_vals).astype(jnp.bfloat16)
    down_part = jnp.einsum(
        "tf,of->to", activated, mlp_mat[:, 2], preferred_element_type=jnp.float32
    )
    mlp_out = lax.psum(down_part.astype(jnp.bfloat16), "tensor").astype(jnp.float32)
    result = (hidden + mlp_out).astype(jnp.bfloat16)
    gain_in, attn_mat, beta_mat = (
        lax.all_gather(gain_in_low, "dp", axis=0, tiled=True),
        lax.all_gather(attn_low, "dp", axis=0, tiled=True),
        lax.all_gather(beta_low, "dp", axis=0, tiled=True),
    )
    gain_mid, mlp_mat = (
        lax.all_gather(gain_mid_low, "dp", axis=0, tiled=True),
        lax.all_gather(mlp_low, "dp", axis=0, tiled=True),
    )
    grad_act = jnp.einsum("to,of->tf", cotangent, mlp_mat[:, 2], preferred_element_type=jnp.float32)
    gate_sig = jax.nn.sigmoid(gate_vals)
    grad_gate = grad_act * up_vals * gate_sig * (1.0 + gate_vals * (1.0 - gate_sig))
    grad_up = grad_act * gate_vals * gate_sig
    grad_gate_up = jnp.stack([grad_gate, grad_up], axis=1).astype(jnp.bfloat16)
    normed_rows = normed_mlp
    grad_rows = cotangent
    first_part = jnp.einsum(
        "tc,tgf->cgf", normed_rows, grad_gate_up, preferred_element_type=jnp.float32
    )
    last_part = jnp.einsum("tc,tf->cf", grad_rows, activated, preferred_element_type=jnp.float32)
    mlp_grad = lax.psum_scatter(
        jnp.concatenate([first_part, last_part[:, None]], axis=1),
        "dp",
        scatter_dimension=0,
        tiled=True,
    )
    grad_normed_mlp_part = jnp.einsum(
        "tgf,dgf->td", grad_gate_up, mlp_mat[:, :2], preferred_element_type=jnp.float32
    )
    grad_normed_mlp = lax.psum(grad_normed_mlp_part.astype(jnp.bfloat16), "tensor").astype(
        jnp.float32
    )
    normed_again, mid_pull = jax.vjp(norm_apply, hidden, gain_mid.astype(jnp.float32))
    grad_hidden_norm, grad_gain_mid = mid_pull(grad_normed_mlp)
    grad_hidden = cotangent.astype(jnp.float32) + grad_hidden_norm
    grad_hidden_low = grad_hidden.astype(jnp.bfloat16)
    grad_mixed = jnp.einsum(
        "to,oc->tc", grad_hidden_low, attn_mat[:, 3], preferred_element_type=jnp.float32
    )
    grad_proj, grad_logits, grad_conv, grad_gain_heads = mixer_pull(grad_mixed)
    grad_proj_low = grad_proj.reshape(length, 3, local_width).astype(jnp.bfloat16)
    grad_logits_low = grad_logits.astype(jnp.bfloat16)
    normed_rows = normed
    grad_rows = grad_hidden_low
    first_part = jnp.einsum(
        "tc,tpe->cpe", normed_rows, grad_proj_low, preferred_element_type=jnp.float32
    )
    last_part = jnp.einsum("tc,te->ce", grad_rows, mixed_low, preferred_element_type=jnp.float32)
    attn_grad = lax.psum_scatter(
        jnp.concatenate([first_part, last_part[:, None]], axis=1),
        "dp",
        scatter_dimension=0,
        tiled=True,
    )
    grad_beta = jnp.einsum("td,th->dh", normed, grad_logits_low, preferred_element_type=jnp.float32)
    grad_normed_part = jnp.einsum(
        "tpe,dpe->td", grad_proj_low, attn_mat[:, :3], preferred_element_type=jnp.float32
    )
    grad_normed_part = grad_normed_part + jnp.einsum(
        "th,dh->td", grad_logits_low, beta_mat, preferred_element_type=jnp.float32
    )
    grad_normed, grad_gain_heads = (
        lax.psum(grad_normed_part.astype(jnp.bfloat16), "tensor").astype(jnp.float32),
        lax.psum(grad_gain_heads.astype(jnp.bfloat16), "tensor").astype(jnp.float32),
    )
    normed_first, in_pull = jax.vjp(norm_apply, inputs_f, gain_in.astype(jnp.float32))
    grad_inputs_norm, grad_gain_in = in_pull(grad_normed)
    grad_inputs = grad_hidden + grad_inputs_norm
    small_sums = (
        lax.psum_scatter(grad_gain_in, "dp", scatter_dimension=0, tiled=True),
        lax.psum_scatter(grad_beta, "dp", scatter_dimension=0, tiled=True),
        lax.psum_scatter(grad_conv, "dp", scatter_dimension=3, tiled=True),
        lax.psum_scatter(grad_gain_heads, "dp", scatter_dimension=0, tiled=True),
        lax.psum_scatter(grad_gain_mid, "dp", scatter_dimension=0, tiled=True),
    )
    return (
        result,
        grad_inputs,
        small_sums[0],
        attn_grad,
        small_sums[1],
        small_sums[2],
        small_sums[3],
        small_sums[4],
        mlp_grad,
    )


def solution(mesh):
    return jax.shard_map(
        body,
        mesh=mesh,
        in_specs=(
            P("dp", None),
            P("dp", None),
            P("dp", None),
            P("dp"),
            P("dp", None, "tensor"),
            P("dp", "tensor"),
            P(None, None, "tensor", "dp"),
            P("dp"),
            P("dp"),
            P("dp", None, "tensor"),
        ),
        out_specs=(
            P("dp", None),
            P("dp", None),
            P("dp"),
            P("dp", None, "tensor"),
            P("dp", "tensor"),
            P(None, None, "tensor", "dp"),
            P("dp"),
            P("dp"),
            P("dp", None, "tensor"),
        ),
        check_vma=False,
    )
```

profile of v0, /device:TPU:0, one launch (start us, length us, event | category | flops | bytes accessed | tf_op | source)
XLA Modules:
  0.0 2766.3 jit_solution(18114808187447301338)
XLA Ops:
  12.9 36.1 %all-reduce.38 = bf16[128]{0:T(256)(128)(2,1)S(1)} all-reduce(bf16[128]{0:T(256)(128)(2,1)S(1)} %dynamic-update-slice), channel_id=1, replica_groups=mesh['dp'=16,'tensor'=2] {'dp'}, use_global_device_ids=true, to_apply=%add.38 | all-reduce | flops 128 | bytes 512
  89.2 20.9 all_gather.29
  111.8 33.6 %all-gather.5.cloned.1.call-done = bf16[2048,4,1024]{2,0,1:T(8,128)(2,1)} async-done(((bf16[128,4,1024]{2,0,1:T(8,128)(2,1)}), bf16[2048,4,1024]{2,0,1:T(8,128)(2,1)}) %all-gather.5.cloned.1.call-update) | async-done | bytes 16777232 | tf_op jit(solution)/shard_map/all_gather | solution.py:134
  201.9 432.9 %while.38 = (s32[]{:T(128)}, f32[8,128,128]{2,1,0:T(8,128)S(1)}, f32[8,64,8,128]{3,1,2,0:T(8,128)}, f32[8,8,128,128]{3,2,1,0:T(8,128)}, s32[8,64]{1,0:T(8,128)S(...) while((s32[]{:T(128)}, f32[8,128,128]{2,1,0:T(8,128)S(1)}, ...), condition=%wide.region_4.6_spmd.clone, body=%wide.region_3.5_spmd.clone.sunk | while | flops 504746240 | bytes 7759869 | solution.py:81
  205.8 39.3 %custom-call.24 = f32[8,1,64,64]{2,3,1,0:T(8,128)S(1)} custom-call(f32[8,1,64,64]{3,2,1,0:T(8,128)S(1)} %fusion.307), custom_call_target="InvertDiagBlocksLowerTriangular" | custom-call | tf_op jit(solution)/shard_map/jvp()/while/body/eval_jaxpr/triangular_solve/custom-call.1 | solution.py:53
  259.9 39.3 %custom-call.24 = f32[8,1,64,64]{2,3,1,0:T(8,128)S(1)} custom-call(f32[8,1,64,64]{3,2,1,0:T(8,128)S(1)} %fusion.307), custom_call_target="InvertDiagBlocksLowerTriangular" | custom-call | tf_op jit(solution)/shard_map/jvp()/while/body/eval_jaxpr/triangular_solve/custom-call.1 | solution.py:53
  314.0 39.3 %custom-call.24 = f32[8,1,64,64]{2,3,1,0:T(8,128)S(1)} custom-call(f32[8,1,64,64]{3,2,1,0:T(8,128)S(1)} %fusion.307), custom_call_target="InvertDiagBlocksLowerTriangular" | custom-call | tf_op jit(solution)/shard_map/jvp()/while/body/eval_jaxpr/triangular_solve/custom-call.1 | solution.py:53
  368.1 39.3 %custom-call.24 = f32[8,1,64,64]{2,3,1,0:T(8,128)S(1)} custom-call(f32[8,1,64,64]{3,2,1,0:T(8,128)S(1)} %fusion.307), custom_call_target="InvertDiagBlocksLowerTriangular" | custom-call | tf_op jit(solution)/shard_map/jvp()/while/body/eval_jaxpr/triangular_solve/custom-call.1 | solution.py:53
  422.2 39.3 %custom-call.24 = f32[8,1,64,64]{2,3,1,0:T(8,128)S(1)} custom-call(f32[8,1,64,64]{3,2,1,0:T(8,128)S(1)} %fusion.307), custom_call_target="InvertDiagBlocksLowerTriangular" | custom-call | tf_op jit(solution)/shard_map/jvp()/while/body/eval_jaxpr/triangular_solve/custom-call.1 | solution.py:53
  476.3 39.3 %custom-call.24 = f32[8,1,64,64]{2,3,1,0:T(8,128)S(1)} custom-call(f32[8,1,64,64]{3,2,1,0:T(8,128)S(1)} %fusion.307), custom_call_target="InvertDiagBlocksLowerTriangular" | custom-call | tf_op jit(solution)/shard_map/jvp()/while/body/eval_jaxpr/triangular_solve/custom-call.1 | solution.py:53
  530.4 39.3 %custom-call.24 = f32[8,1,64,64]{2,3,1,0:T(8,128)S(1)} custom-call(f32[8,1,64,64]{3,2,1,0:T(8,128)S(1)} %fusion.307), custom_call_target="InvertDiagBlocksLowerTriangular" | custom-call | tf_op jit(solution)/shard_map/jvp()/while/body/eval_jaxpr/triangular_solve/custom-call.1 | solution.py:53
  584.5 39.3 %custom-call.24 = f32[8,1,64,64]{2,3,1,0:T(8,128)S(1)} custom-call(f32[8,1,64,64]{3,2,1,0:T(8,128)S(1)} %fusion.307), custom_call_target="InvertDiagBlocksLowerTriangular" | custom-call | tf_op jit(solution)/shard_map/jvp()/while/body/eval_jaxpr/triangular_solve/custom-call.1 | solution.py:53
  684.3 67.2 %all-reduce.50.cloned.1.call-done = f32[512,2048]{1,0:T(8,128)} async-done(((f32[512,2048]{1,0:T(8,128)}), f32[512,2048]{1,0:T(8,128)}) %all-reduce.50.cloned.1.call-update) | async-done | bytes 4194320 | tf_op jit(solution)/shard_map/psum | solution.py:173
  756.2 170.0 %all-gather.7.cloned.1.call-done = bf16[2048,3,2816]{2,0,1:T(8,128)(2,1)} async-done(((bf16[128,3,2816]{2,0,1:T(8,128)(2,1)}), bf16[2048,3,2816]{2,0,1:T(8,128)(2,1)}) %all-gather.7.cloned.1.call-update) | async-done | bytes 34603024 | tf_op jit(solution)/shard_map/all_gather | solution.py:141
  926.2 20.5 fusion.86
  996.0 47.1 %all-reduce.52.cloned.1.call-done = bf16[512,2048]{1,0:T(8,128)(2,1)} async-done(((bf16[512,2048]{1,0:T(8,128)(2,1)}), bf16[512,2048]{1,0:T(8,128)(2,1)}) %all-reduce.52.cloned.1.call-update) | async-done | bytes 2097168 | tf_op jit(solution)/shard_map/psum | solution.py:216
  1062.7 495.5 %while.39 = (s32[]{:T(128)}, f32[8,128,128]{2,1,0:T(8,128)S(1)}, f32[8,64,8,128]{3,1,0,2:T(8,128)}, f32[8,64,8,128]{3,1,0,2:T(8,128)}, f32[8,64,8,128]{3,1,0,2:T...) while((s32[]{:T(128)}, f32[8,128,128]{2,1,0:T(8,128)S(1)}, ...), condition=%wide.region_15.17_spmd.clone, body=%wide.region_12.16_spmd.clone.sunk | while | flops 1285967616 | bytes 23183872 | solution.py:81
  1071.0 39.3 %custom-call.25 = f32[8,1,64,64]{2,3,1,0:T(8,128)S(1)} custom-call(f32[8,1,64,64]{3,2,1,0:T(8,128)S(1)} %add_bitcast_fusion.8), custom_call_target="InvertDiagBlocksLowerTriangular" | custom-call | tf_op jit(solution)/shard_map/transpose(jvp())/while/body/eval_jaxpr/checkpoint/triangular_solve | solution.py:53
  1132.9 39.3 %custom-call.25 = f32[8,1,64,64]{2,3,1,0:T(8,128)S(1)} custom-call(f32[8,1,64,64]{3,2,1,0:T(8,128)S(1)} %add_bitcast_fusion.8), custom_call_target="InvertDiagBlocksLowerTriangular" | custom-call | tf_op jit(solution)/shard_map/transpose(jvp())/while/body/eval_jaxpr/checkpoint/triangular_solve | solution.py:53
  1194.8 39.3 %custom-call.25 = f32[8,1,64,64]{2,3,1,0:T(8,128)S(1)} custom-call(f32[8,1,64,64]{3,2,1,0:T(8,128)S(1)} %add_bitcast_fusion.8), custom_call_target="InvertDiagBlocksLowerTriangular" | custom-call | tf_op jit(solution)/shard_map/transpose(jvp())/while/body/eval_jaxpr/checkpoint/triangular_solve | solution.py:53
  1256.7 39.3 %custom-call.25 = f32[8,1,64,64]{2,3,1,0:T(8,128)S(1)} custom-call(f32[8,1,64,64]{3,2,1,0:T(8,128)S(1)} %add_bitcast_fusion.8), custom_call_target="InvertDiagBlocksLowerTriangular" | custom-call | tf_op jit(solution)/shard_map/transpose(jvp())/while/body/eval_jaxpr/checkpoint/triangular_solve | solution.py:53
  1318.6 39.3 %custom-call.25 = f32[8,1,64,64]{2,3,1,0:T(8,128)S(1)} custom-call(f32[8,1,64,64]{3,2,1,0:T(8,128)S(1)} %add_bitcast_fusion.8), custom_call_target="InvertDiagBlocksLowerTriangular" | custom-call | tf_op jit(solution)/shard_map/transpose(jvp())/while/body/eval_jaxpr/checkpoint/triangular_solve | solution.py:53
  1380.4 39.3 %custom-call.25 = f32[8,1,64,64]{2,3,1,0:T(8,128)S(1)} custom-call(f32[8,1,64,64]{3,2,1,0:T(8,128)S(1)} %add_bitcast_fusion.8), custom_call_target="InvertDiagBlocksLowerTriangular" | custom-call | tf_op jit(solution)/shard_map/transpose(jvp())/while/body/eval_jaxpr/checkpoint/triangular_solve | solution.py:53
  1442.3 39.3 %custom-call.25 = f32[8,1,64,64]{2,3,1,0:T(8,128)S(1)} custom-call(f32[8,1,64,64]{3,2,1,0:T(8,128)S(1)} %add_bitcast_fusion.8), custom_call_target="InvertDiagBlocksLowerTriangular" | custom-call | tf_op jit(solution)/shard_map/transpose(jvp())/while/body/eval_jaxpr/checkpoint/triangular_solve | solution.py:53
  1504.1 39.3 %custom-call.25 = f32[8,1,64,64]{2,3,1,0:T(8,128)S(1)} custom-call(f32[8,1,64,64]{3,2,1,0:T(8,128)S(1)} %add_bitcast_fusion.8), custom_call_target="InvertDiagBlocksLowerTriangular" | custom-call | tf_op jit(solution)/shard_map/transpose(jvp())/while/body/eval_jaxpr/checkpoint/triangular_solve | solution.py:53
  1622.7 20.6 pad_maximum_fusion.1
  1659.8 25.2 fusion.116
  1686.4 49.2 %pad_maximum_fusion = f32[2048,3,2816]{2,0,1:T(8,128)} fusion(f32[2048,1,2816]{2,0,1:T(8,128)} %convolution_bitcast_fusion.5, f32[2048,2,2816]{2,0,1:T(8,128)} %fusion.116), kind=kLoop, calls=%fused_computation.142 | loop fusion | flops 17301504 | bytes 138412032 | tf_op jit(solution)/shard_map/concatenate | solution.py:208
  1746.1 63.7 %all-reduce.55 = (f32[2048]{0:T(1024)S(1)}, f32[3,4,8,128]{3,2,1,0:T(8,128)S(1)}, f32[128]{0:T(128)S(1)}, f32[2048]{0:T(1024)S(1)}) all-reduce(f32[2048]{0:T(1024)S(1)} %get-tuple-element.569, f32[3,4,8,128]{3,2,1,0:T(8,128)S(1)} %pad_add_fusion, bf16[128]{0:T(256)(128)(2,1)S(1)} %psum.39, ...), channel_id=2, replica_groups=mesh['dp'=16,'tensor'=2] {'dp'}, use_global_device_ids=true, to_apply=%region_21.23.clone | all-reduce | flops 16512 | bytes 131840
  1820.5 224.0 %reduce-scatter.5.cloned.1.call-done = f32[128,4,1024]{2,0,1:T(8,128)} async-done(((f32[2048,4,1024]{2,0,1:T(8,128)}), f32[128,4,1024]{2,0,1:T(8,128)}) %reduce-scatter.5.cloned.1.call-update) | async-done | bytes 2097168 | tf_op jit(solution)/shard_map/reduce_scatter | solution.py:235
  2048.7 51.1 %reduce-scatter.7.cloned.1.call-done = f32[128,8]{0,1:T(8,128)} async-done(((f32[2048,8]{0,1:T(8,128)}), f32[128,8]{0,1:T(8,128)}) %reduce-scatter.7.cloned.1.call-update) | async-done | bytes 4112 | tf_op jit(solution)/shard_map/reduce_scatter | solution.py:257
  2099.8 659.4 %reduce-scatter.9.cloned.1.call-done = f32[128,3,2816]{2,0,1:T(8,128)} async-done(((f32[2048,3,2816]{2,0,1:T(8,128)}), f32[128,3,2816]{2,0,1:T(8,128)}) %reduce-scatter.9.cloned.1.call-update) | async-done | bytes 4325392 | tf_op jit(solution)/shard_map/reduce_scatter | solution.py:207
  (809 shorter events, 627.9 us)
Async XLA Ops:
  7.2 60.1 %copy-start.52 = (f32[3,4,8,8]{3,2,1,0:T(8,128)S(1)}, f32[3,4,8,8]{3,2,1,0:T(8,128)}, u32[]{:S(2)}) copy-start(f32[3,4,8,8]{3,2,1,0:T(8,128)} %param.22) | copy-start | bytes 9220
  7.2 80.0 %copy-start.6 = (bf16[512,2048]{1,0:T(8,128)(2,1)S(1)}, bf16[512,2048]{1,0:T(8,128)(2,1)}, u32[]{:S(2)}) copy-start(bf16[512,2048]{1,0:T(8,128)(2,1)} %param.16) | copy-start | bytes 6291460
  7.3 138.2 %all-gather.5.cloned.1.call-start = ((), (), s32[]{:S(2)}) async-start(), calls=%async_computation.3 | async-start | bytes 17825792 | tf_op jit(solution)/shard_map/all_gather | solution.py:134
  11.2 740.4 %all-reduce.50.cloned.1.call-start = ((), (), s32[]{:S(2)}) async-start(), calls=%async_computation.4 | async-start | bytes 8388608 | tf_op jit(solution)/shard_map/psum | solution.py:173
  67.3 105.6 %copy-start.39 = (f32[16,1,128]{2,1,0:T(1,128)}, f32[16,1,128]{2,1,0:T(1,128)S(1)}, u32[]{:S(2)}) copy-start(f32[16,1,128]{2,1,0:T(1,128)S(1)} %convert_element_type.232) | copy-start | bytes 24580
  87.8 85.2 %copy-start.78 = (f32[512]{0:T(512)}, f32[512]{0:T(512)S(1)}, u32[]{:S(2)}) copy-start(f32[512]{0:T(512)S(1)} %fusion.174) | copy-start | bytes 6148
  110.8 81.2 %copy-start.55 = (f32[8,128]{1,0:T(8,128)}, f32[8,128]{1,0:T(8,128)S(1)}, u32[]{:S(2)}) copy-start(f32[8,128]{1,0:T(8,128)S(1)} %copy.108) | copy-start | bytes 12292
  110.9 81.2 %copy-start.65 = (f32[8,128]{1,0:T(8,128)}, f32[8,128]{1,0:T(8,128)S(1)}, u32[]{:S(2)}) copy-start(f32[8,128]{1,0:T(8,128)S(1)} %copy.109) | copy-start | bytes 12292
  110.9 81.1 %copy-start.61 = (f32[8,128]{1,0:T(8,128)}, f32[8,128]{1,0:T(8,128)S(1)}, u32[]{:S(2)}) copy-start(f32[8,128]{1,0:T(8,128)S(1)} %copy.110) | copy-start | bytes 12292
  111.0 81.0 %copy-start.59 = (f32[8,128]{1,0:T(8,128)}, f32[8,128]{1,0:T(8,128)S(1)}, u32[]{:S(2)}) copy-start(f32[8,128]{1,0:T(8,128)S(1)} %copy.111) | copy-start | bytes 12292
  111.1 81.0 %copy-start.53 = (f32[8,128]{1,0:T(8,128)}, f32[8,128]{1,0:T(8,128)S(1)}, u32[]{:S(2)}) copy-start(f32[8,128]{1,0:T(8,128)S(1)} %copy.104) | copy-start | bytes 12292
  111.2 80.9 %copy-start.71 = (f32[8,128]{1,0:T(8,128)}, f32[8,128]{1,0:T(8,128)S(1)}, u32[]{:S(2)}) copy-start(f32[8,128]{1,0:T(8,128)S(1)} %copy.105) | copy-start | bytes 12292
  111.2 80.8 %copy-start.67 = (f32[8,128]{1,0:T(8,128)}, f32[8,128]{1,0:T(8,128)S(1)}, u32[]{:S(2)}) copy-start(f32[8,128]{1,0:T(8,128)S(1)} %copy.106) | copy-start | bytes 12292
  111.3 80.8 %copy-start.63 = (f32[8,128]{1,0:T(8,128)}, f32[8,128]{1,0:T(8,128)S(1)}, u32[]{:S(2)}) copy-start(f32[8,128]{1,0:T(8,128)S(1)} %copy.107) | copy-start | bytes 12292
  111.4 72.9 %copy-start.57 = (f32[8,128]{1,0:T(8,128)}, f32[8,128]{1,0:T(8,128)S(1)}, u32[]{:S(2)}) copy-start(f32[8,128]{1,0:T(8,128)S(1)} %copy.100) | copy-start | bytes 12292
  111.4 72.9 %copy-start.75 = (f32[8,128]{1,0:T(8,128)}, f32[8,128]{1,0:T(8,128)S(1)}, u32[]{:S(2)}) copy-start(f32[8,128]{1,0:T(8,128)S(1)} %copy.101) | copy-start | bytes 12292
  111.5 72.8 %copy-start.73 = (f32[8,128]{1,0:T(8,128)}, f32[8,128]{1,0:T(8,128)S(1)}, u32[]{:S(2)}) copy-start(f32[8,128]{1,0:T(8,128)S(1)} %copy.102) | copy-start | bytes 12292
  111.6 72.7 %copy-start.69 = (f32[8,128]{1,0:T(8,128)}, f32[8,128]{1,0:T(8,128)S(1)}, u32[]{:S(2)}) copy-start(f32[8,128]{1,0:T(8,128)S(1)} %copy.103) | copy-start | bytes 12292
  111.7 537.5 %copy-start.46 = (f32[512]{0:T(512)}, f32[512]{0:T(512)S(1)}, u32[]{:S(2)}) copy-start(f32[512]{0:T(512)S(1)} %get-tuple-element.697) | copy-start | bytes 6148
  111.7 538.1 %copy-start.48 = (f32[512]{0:T(512)}, f32[512]{0:T(512)S(1)}, u32[]{:S(2)}) copy-start(f32[512]{0:T(512)S(1)} %get-tuple-element.698) | copy-start | bytes 6148
  111.7 538.8 %copy-start.50 = (f32[512]{0:T(512)}, f32[512]{0:T(512)S(1)}, u32[]{:S(2)}) copy-start(f32[512]{0:T(512)S(1)} %get-tuple-element.699) | copy-start | bytes 6148
  645.3 280.9 %all-gather.7.cloned.1.call-start = ((), (), s32[]{:S(2)}) async-start(), calls=%async_computation.5 | async-start | bytes 36765696 | tf_op jit(solution)/shard_map/all_gather | solution.py:141
  649.2 393.9 %all-reduce.52.cloned.1.call-start = ((), (), s32[]{:S(2)}) async-start(), calls=%async_computation.6 | async-start | bytes 4194304 | tf_op jit(solution)/shard_map/psum | solution.py:216
  669.5 378.5 %copy-start.41 = (f32[16,1,128]{2,1,0:T(1,128)}, f32[16,1,128]{2,1,0:T(1,128)S(1)}, u32[]{:S(2)}) copy-start(f32[16,1,128]{2,1,0:T(1,128)S(1)} %convert_element_type.233) | copy-start | bytes 24580
  756.2 291.7 %copy-start.80 = (f32[512]{0:T(512)}, f32[512]{0:T(512)S(1)}, u32[]{:S(2)}) copy-start(f32[512]{0:T(512)S(1)} %fusion.175) | copy-start | bytes 6148
  980.0 762.4 %all-reduce.54.cloned.1.call-start = ((), (), s32[]{:S(2)}) async-start(), calls=%async_computation.10 | async-start | bytes 8388608 | tf_op jit(solution)/shard_map/psum | solution.py:185
  1062.7 495.6 %copy-start.44 = (f32[512,8]{0,1:T(8,128)S(1)}, f32[512,8]{0,1:T(8,128)}, u32[]{:S(2)}) copy-start(f32[512,8]{0,1:T(8,128)} %copy-done.43) | copy-start | bytes 49156
  1062.7 500.5 %copy-start.36 = (f32[512,8]{0,1:T(8,128)S(1)}, f32[512,8]{0,1:T(8,128)}, u32[]{:S(2)}) copy-start(f32[512,8]{0,1:T(8,128)} %copy-done.35) | copy-start | bytes 49156
  1598.1 446.4 %reduce-scatter.5.cloned.1.call-start = ((), (), s32[]{:S(2)}) async-start(), calls=%async_computation.7 | async-start | bytes 35651584 | tf_op jit(solution)/shard_map/reduce_scatter | solution.py:235
  1643.4 456.4 %reduce-scatter.7.cloned.1.call-start = ((), (), s32[]{:S(2)}) async-start(), calls=%async_computation.8 | async-start | bytes 69632 | tf_op jit(solution)/shard_map/reduce_scatter | solution.py:257
  1686.3 1072.9 %reduce-scatter.9.cloned.1.call-start = ((), (), s32[]{:S(2)}) async-start(), calls=%async_computation.9 | async-start | bytes 73531392 | tf_op jit(solution)/shard_map/reduce_scatter | solution.py:207
  1742.4 69.8 %copy-start.83 = (f32[512]{0:T(512)S(1)}, f32[512]{0:T(512)}, u32[]{:S(2)}) copy-start(f32[512]{0:T(512)} %copy-done.82) | copy-start | bytes 6148
  (81 other events, 529.6 us)
Sparse Core Ops, SparseCore 0:
  11.3 134.1 all-gather.4
  645.4 106.0 all-reduce.49
  753.2 172.9 all-gather.6
  980.1 62.9 all-reduce.51
  1598.2 108.2 all-reduce.53
  1711.2 333.2 reduce-scatter.4
  2048.8 50.9 reduce-scatter.6
  2104.6 654.5 reduce-scatter.8
where the time goes:
time: 2770 us
  waiting for transfers between devices  1250 us (45%)
  other arithmetic  788 us (28%)
  matrix products  384 us (14%)
  blocking collectives  181 us (7%)
  local copies, waits for them, and re-layouts  140 us (5%)
    reduce_scatter x2, waiting for transfers between devices, body(): lax.psum_scatter(jnp.concatenate([first_part, last_part[:, None]], axis=1...  883 us
    another operation x64, other arithmetic, delta_block(): lax.linalg.triangular_solve(system, target, left_side=True, lower=True, u...  632 us
    all_gather x1, waiting for transfers between devices, body(): lax.all_gather(mlp_low, 'dp', axis=0, tiled=True)  170 us
    unnamed x2, blocking collectives  99.7 us
    concatenate x2, other arithmetic, body(): jnp.concatenate([first_part, last_part[:, None]], axis=1)  69.9 us
    psum x1, waiting for transfers between devices, body(): attended = lax.psum(attn_part, 'tensor')  67.2 us
  transfers between devices with their start and end apart: 8, of which 7 were waited for; matrix products, arithmetic and copies ran while one was open for 7% of the time, Pallas kernels for 0%

commit v1 on v0

--- a/solution.py
+++ b/solution.py
@@ -5,6 +5,27 @@
 
 BLOCK = 64
 highest = lax.Precision.HIGHEST
+
+
+def joined_along(blocks, dim):
+    blocks = jnp.moveaxis(blocks, 0, dim)
+    shape = blocks.shape
+    return blocks.reshape(*shape[:dim], shape[dim] * shape[dim + 1], *shape[dim + 2 :])
+
+
+def grow_blocks(shard, axis):
+    length, position = (lax.axis_size(axis), lax.axis_index(axis))
+    blocks, bit = (shard[None], 1)
+    while bit < length:
+        other = lax.ppermute(blocks, axis, [(i, i ^ bit) for i in range(length)])
+        low = position & bit == 0
+        blocks = jnp.concatenate([jnp.where(low, blocks, other), jnp.where(low, other, blocks)])
+        bit *= 2
+    return blocks
+
+
+def gather_by_bits(value, axis, dim):
+    return joined_along(grow_blocks(value, axis), dim)
 
 
 def rms_scale(values, gain_values, epsilon):
@@ -138,7 +159,7 @@
     )
     gain_mid, mlp_mat = (
         lax.all_gather(gain_mid_low, "dp", axis=0, tiled=True),
-        lax.all_gather(mlp_low, "dp", axis=0, tiled=True),
+        gather_by_bits(mlp_low, "dp", 0),
     )
     model_width = attn_mat.shape[0]
     local_width = attn_mat.shape[2]

time: 2770 us -> 3880 us (1.40)
  waiting for transfers between devices: 1250 us -> 1810 us
  blocking collectives: 181 us -> 547 us
  other arithmetic: 788 us -> 906 us
  local copies, waits for them, and re-layouts: 140 us -> 188 us
    ppermute x0 -> x4, waiting for transfers between devices: none -> 773 us  [grow_blocks(): other = lax.ppermute(blocks, axis, [(i, i ^ bit) for i in range(length)])]
    all_gather x1, blocking collectives: 18.3 us -> 384 us  [body(): lax.all_gather(gain_mid_low, 'dp', axis=0, tiled=True)]
    all_gather x1, waiting for transfers between devices: 170 us -> 0.01 us  [body(): lax.all_gather(mlp_low, 'dp', axis=0, tiled=True)]
    psum x1, waiting for transfers between devices: 67.2 us -> 0.01 us  [body(): attended = lax.psum(attn_part, 'tensor')]
    concatenate x0 -> x4, other arithmetic: none -> 44.4 us  [grow_blocks(): jnp.concatenate([jnp.where(low, blocks, other), jnp.where(low, other, blo...]
    select_n x0 -> x4, other arithmetic: none -> 39.6 us  [grow_blocks(): jnp.where(low, blocks, other)]
  transfers between devices with their start and end apart: 8 -> 12, of which waited for: 7 -> 9; matrix products, arithmetic and copies ran while one was open for 7% -> 9% of each run, Pallas kernels for 0% -> 0%
where the time goes in v1:
time: 3880 us; the launch traced here: 3870 us
  waiting for transfers between devices  1810 us (47%)
  other arithmetic  906 us (23%)
  blocking collectives  547 us (14%)
  matrix products  395 us (10%)
  local copies, waits for them, and re-layouts  188 us (5%)
    reduce_scatter x2, waiting for transfers between devices, body(): lax.psum_scatter(jnp.concatenate([first_part, last_part[:, None]], axis=1...  883 us
    ppermute x4, waiting for transfers between devices, grow_blocks(): other = lax.ppermute(blocks, axis, [(i, i ^ bit) for i in range(length)])  773 us
    another operation x64, other arithmetic, delta_block(): lax.linalg.triangular_solve(system, target, left_side=True, lower=True, u...  649 us
    all_gather x1, blocking collectives, body(): lax.all_gather(gain_mid_low, 'dp', axis=0, tiled=True)  384 us
    unnamed x2, blocking collectives  95.2 us
  transfers between devices with their start and end apart: 12, of which 9 were waited for; matrix products, arithmetic and copies ran while one was open for 9% of the time, Pallas kernels for 0%

profile of v1, /device:TPU:0, one launch (start us, length us, event | category | flops | bytes accessed | tf_op | source)
XLA Modules:
  0.0 3872.8 jit_solution(2989332917904533534)
XLA Ops:
  80.4 31.5 all-reduce.38
  112.5 30.3 all-gather.5.cloned.1.call-done
  199.3 455.4 %while.38 = (s32[]{:T(128)}, f32[8,128,128]{2,1,0:T(8,128)S(1)}, f32[8,64,8,128]{3,1,2,0:T(8,128)}, f32[8,8,128,128]{3,2,1,0:T(8,128)}, s32[8,64]{1,0:T(8,128)},...) while((s32[]{:T(128)}, f32[8,128,128]{2,1,0:T(8,128)S(1)}, ...), condition=%wide.region_4.6_spmd.clone, body=%wide.region_3.5_spmd.clone.sunk | while | flops 504746240 | bytes 7759869 | solution.py:102
  210.0 40.0 %custom-call.24 = f32[8,1,64,64]{2,3,1,0:T(8,128)S(1)} custom-call(f32[8,1,64,64]{3,2,1,0:T(8,128)} %fusion.307), custom_call_target="InvertDiagBlocksLowerTriangular" | custom-call | tf_op jit(solution)/shard_map/jvp()/while/body/eval_jaxpr/triangular_solve/custom-call.1 | solution.py:74
  266.8 40.0 %custom-call.24 = f32[8,1,64,64]{2,3,1,0:T(8,128)S(1)} custom-call(f32[8,1,64,64]{3,2,1,0:T(8,128)} %fusion.307), custom_call_target="InvertDiagBlocksLowerTriangular" | custom-call | tf_op jit(solution)/shard_map/jvp()/while/body/eval_jaxpr/triangular_solve/custom-call.1 | solution.py:74
  323.7 40.0 %custom-call.24 = f32[8,1,64,64]{2,3,1,0:T(8,128)S(1)} custom-call(f32[8,1,64,64]{3,2,1,0:T(8,128)} %fusion.307), custom_call_target="InvertDiagBlocksLowerTriangular" | custom-call | tf_op jit(solution)/shard_map/jvp()/while/body/eval_jaxpr/triangular_solve/custom-call.1 | solution.py:74
  380.6 40.0 %custom-call.24 = f32[8,1,64,64]{2,3,1,0:T(8,128)S(1)} custom-call(f32[8,1,64,64]{3,2,1,0:T(8,128)} %fusion.307), custom_call_target="InvertDiagBlocksLowerTriangular" | custom-call | tf_op jit(solution)/shard_map/jvp()/while/body/eval_jaxpr/triangular_solve/custom-call.1 | solution.py:74
  437.4 40.0 %custom-call.24 = f32[8,1,64,64]{2,3,1,0:T(8,128)S(1)} custom-call(f32[8,1,64,64]{3,2,1,0:T(8,128)} %fusion.307), custom_call_target="InvertDiagBlocksLowerTriangular" | custom-call | tf_op jit(solution)/shard_map/jvp()/while/body/eval_jaxpr/triangular_solve/custom-call.1 | solution.py:74
  494.3 40.0 %custom-call.24 = f32[8,1,64,64]{2,3,1,0:T(8,128)S(1)} custom-call(f32[8,1,64,64]{3,2,1,0:T(8,128)} %fusion.307), custom_call_target="InvertDiagBlocksLowerTriangular" | custom-call | tf_op jit(solution)/shard_map/jvp()/while/body/eval_jaxpr/triangular_solve/custom-call.1 | solution.py:74
  551.1 40.0 %custom-call.24 = f32[8,1,64,64]{2,3,1,0:T(8,128)S(1)} custom-call(f32[8,1,64,64]{3,2,1,0:T(8,128)} %fusion.307), custom_call_target="InvertDiagBlocksLowerTriangular" | custom-call | tf_op jit(solution)/shard_map/jvp()/while/body/eval_jaxpr/triangular_solve/custom-call.1 | solution.py:74
  608.0 40.0 %custom-call.24 = f32[8,1,64,64]{2,3,1,0:T(8,128)S(1)} custom-call(f32[8,1,64,64]{3,2,1,0:T(8,128)} %fusion.307), custom_call_target="InvertDiagBlocksLowerTriangular" | custom-call | tf_op jit(solution)/shard_map/jvp()/while/body/eval_jaxpr/triangular_solve/custom-call.1 | solution.py:74
  685.9 94.4 %collective-permute-done.1 = bf16[2,128,3,2816]{3,1,2,0:T(8,128)(2,1)} collective-permute-done((bf16[2,128,3,2816]{3,1,2,0:T(8,128)(2,1)}, bf16[2,128,3,2816]{3,1,2,0:T(8,128)(2,1)}, u32[]{:S(2)}, u32[]{:S(2)}) %collective-permute-start.1) | collective-permute-done | bytes 4325408 | tf_op jit(solution)/shard_map/ppermute | solution.py:20
  796.3 333.4 %collective-permute-done.2 = bf16[4,128,3,2816]{3,1,2,0:T(8,128)(2,1)} collective-permute-done((bf16[4,128,3,2816]{3,1,2,0:T(8,128)(2,1)}, bf16[4,128,3,2816]{3,1,2,0:T(8,128)(2,1)}, u32[]{:S(2)}, u32[]{:S(2)}) %collective-permute-start.2) | collective-permute-done | bytes 8650784 | tf_op jit(solution)/shard_map/ppermute | solution.py:20
  1151.8 384.4 %all-gather.1 = bf16[16,1,128]{2,1,0:T(2,128)(2,1)S(1)} all-gather(bf16[1,1,128]{2,1,0:T(2,128)(2,1)S(1)} %convert_bitcast_fusion.1), channel_id=1, replica_groups=mesh['dp'=16,'tensor'=2] {'dp'}, dimensions={0}, use_global_device_ids=true | all-gather | bytes 4352 | tf_op jit(solution)/shard_map/all_gather | solution.py:161
  1551.2 341.3 %collective-permute-done.3 = bf16[8,128,3,2816]{3,1,2,0:T(8,128)(2,1)} collective-permute-done((bf16[8,128,3,2816]{3,1,2,0:T(8,128)(2,1)}, bf16[8,128,3,2816]{3,1,2,0:T(8,128)(2,1)}, u32[]{:S(2)}, u32[]{:S(2)}) %collective-permute-start.3) | collective-permute-done | bytes 17301536 | tf_op jit(solution)/shard_map/ppermute | solution.py:20
  1915.7 23.9 pad_maximum_fusion.1
  2037.4 71.6 %all-reduce.52.cloned.1.call-done = bf16[512,2048]{1,0:T(8,128)(2,1)} async-done(((bf16[512,2048]{1,0:T(8,128)(2,1)}), bf16[512,2048]{1,0:T(8,128)(2,1)}) %all-reduce.52.cloned.1.call-update) | async-done | bytes 2097168 | tf_op jit(solution)/shard_map/psum | solution.py:237
  2128.6 536.0 %while.39 = (s32[]{:T(128)}, f32[8,128,128]{2,1,0:T(8,128)}, f32[8,64,8,128]{3,1,0,2:T(8,128)}, f32[8,64,8,128]{3,1,0,2:T(8,128)}, f32[8,64,8,128]{3,1,0,2:T(8,1...) while((s32[]{:T(128)}, f32[8,128,128]{2,1,0:T(8,128)}, ...), condition=%wide.region_15.17_spmd.clone, body=%wide.region_12.16_spmd.clone.sunk | while | flops 1285967616 | bytes 23185976 | solution.py:102
  2142.5 40.0 %custom-call.25 = f32[8,1,64,64]{2,3,1,0:T(8,128)S(1)} custom-call(f32[8,1,64,64]{3,2,1,0:T(8,128)} %add_bitcast_fusion.8), custom_call_target="InvertDiagBlocksLowerTriangular" | custom-call | tf_op jit(solution)/shard_map/transpose(jvp())/while/body/eval_jaxpr/checkpoint/triangular_solve | solution.py:74
  2209.6 40.0 %custom-call.25 = f32[8,1,64,64]{2,3,1,0:T(8,128)S(1)} custom-call(f32[8,1,64,64]{3,2,1,0:T(8,128)} %add_bitcast_fusion.8), custom_call_target="InvertDiagBlocksLowerTriangular" | custom-call | tf_op jit(solution)/shard_map/transpose(jvp())/while/body/eval_jaxpr/checkpoint/triangular_solve | solution.py:74
  2276.7 40.0 %custom-call.25 = f32[8,1,64,64]{2,3,1,0:T(8,128)S(1)} custom-call(f32[8,1,64,64]{3,2,1,0:T(8,128)} %add_bitcast_fusion.8), custom_call_target="InvertDiagBlocksLowerTriangular" | custom-call | tf_op jit(solution)/shard_map/transpose(jvp())/while/body/eval_jaxpr/checkpoint/triangular_solve | solution.py:74
  2343.8 40.0 %custom-call.25 = f32[8,1,64,64]{2,3,1,0:T(8,128)S(1)} custom-call(f32[8,1,64,64]{3,2,1,0:T(8,128)} %add_bitcast_fusion.8), custom_call_target="InvertDiagBlocksLowerTriangular" | custom-call | tf_op jit(solution)/shard_map/transpose(jvp())/while/body/eval_jaxpr/checkpoint/triangular_solve | solution.py:74
  2410.8 40.0 %custom-call.25 = f32[8,1,64,64]{2,3,1,0:T(8,128)S(1)} custom-call(f32[8,1,64,64]{3,2,1,0:T(8,128)} %add_bitcast_fusion.8), custom_call_target="InvertDiagBlocksLowerTriangular" | custom-call | tf_op jit(solution)/shard_map/transpose(jvp())/while/body/eval_jaxpr/checkpoint/triangular_solve | solution.py:74
  2478.0 40.0 %custom-call.25 = f32[8,1,64,64]{2,3,1,0:T(8,128)S(1)} custom-call(f32[8,1,64,64]{3,2,1,0:T(8,128)} %add_bitcast_fusion.8), custom_call_target="InvertDiagBlocksLowerTriangular" | custom-call | tf_op jit(solution)/shard_map/transpose(jvp())/while/body/eval_jaxpr/checkpoint/triangular_solve | solution.py:74
  2545.1 40.0 %custom-call.25 = f32[8,1,64,64]{2,3,1,0:T(8,128)S(1)} custom-call(f32[8,1,64,64]{3,2,1,0:T(8,128)} %add_bitcast_fusion.8), custom_call_target="InvertDiagBlocksLowerTriangular" | custom-call | tf_op jit(solution)/shard_map/transpose(jvp())/while/body/eval_jaxpr/checkpoint/triangular_solve | solution.py:74
  2612.2 40.0 %custom-call.25 = f32[8,1,64,64]{2,3,1,0:T(8,128)S(1)} custom-call(f32[8,1,64,64]{3,2,1,0:T(8,128)} %add_bitcast_fusion.8), custom_call_target="InvertDiagBlocksLowerTriangular" | custom-call | tf_op jit(solution)/shard_map/transpose(jvp())/while/body/eval_jaxpr/checkpoint/triangular_solve | solution.py:74
  2766.6 25.2 fusion.116
  2793.2 49.1 %pad_maximum_fusion = f32[2048,3,2816]{2,0,1:T(8,128)} fusion(f32[2048,1,2816]{2,0,1:T(8,128)} %convolution_bitcast_fusion.5, f32[2048,2,2816]{2,0,1:T(8,128)} %fusion.116), kind=kLoop, calls=%fused_computation.142 | loop fusion | flops 17301504 | bytes 138412032 | tf_op jit(solution)/shard_map/concatenate | solution.py:229
  2852.8 63.7 %all-reduce.55 = (f32[2048]{0:T(1024)S(1)}, f32[3,4,8,128]{3,2,1,0:T(8,128)S(1)}, f32[128]{0:T(128)S(1)}, f32[2048]{0:T(1024)S(1)}) all-reduce(f32[2048]{0:T(1024)S(1)} %get-tuple-element.569, f32[3,4,8,128]{3,2,1,0:T(8,128)S(1)} %pad_add_fusion, bf16[128]{0:T(256)(128)(2,1)S(1)} %psum.39, ...), channel_id=2, replica_groups=mesh['dp'=16,'tensor'=2] {'dp'}, use_global_device_ids=true, to_apply=%region_21.23.clone | all-reduce | flops 16512 | bytes 131840
  2927.2 224.1 %reduce-scatter.5.cloned.1.call-done = f32[128,4,1024]{2,0,1:T(8,128)} async-done(((f32[2048,4,1024]{2,0,1:T(8,128)}), f32[128,4,1024]{2,0,1:T(8,128)}) %reduce-scatter.5.cloned.1.call-update) | async-done | bytes 2097168 | tf_op jit(solution)/shard_map/reduce_scatter | solution.py:256
  3155.5 50.9 %reduce-scatter.7.cloned.1.call-done = f32[128,8]{0,1:T(8,128)} async-done(((f32[2048,8]{0,1:T(8,128)}), f32[128,8]{0,1:T(8,128)}) %reduce-scatter.7.cloned.1.call-update) | async-done | bytes 4112 | tf_op jit(solution)/shard_map/reduce_scatter | solution.py:278
  3206.4 659.3 %reduce-scatter.9.cloned.1.call-done = f32[128,3,2816]{2,0,1:T(8,128)} async-done(((f32[2048,3,2816]{2,0,1:T(8,128)}), f32[128,3,2816]{2,0,1:T(8,128)}) %reduce-scatter.9.cloned.1.call-update) | async-done | bytes 4325392 | tf_op jit(solution)/shard_map/reduce_scatter | solution.py:228
  (881 shorter events, 827.8 us)
Async XLA Ops:
  7.2 135.6 %all-gather.5.cloned.1.call-start = ((), (), s32[]{:S(2)}) async-start(), calls=%async_computation.3 | async-start | bytes 17825792 | tf_op jit(solution)/shard_map/all_gather | solution.py:155
  11.1 1952.3 %all-reduce.50.cloned.1.call-start = ((), (), s32[]{:S(2)}) async-start(), calls=%async_computation.4 | async-start | bytes 8388608 | tf_op jit(solution)/shard_map/psum | solution.py:194
  36.3 134.1 %copy-start.47 = (f32[16,1,128]{2,1,0:T(1,128)}, f32[16,1,128]{2,1,0:T(1,128)S(1)}, u32[]{:S(2)}) copy-start(f32[16,1,128]{2,1,0:T(1,128)S(1)} %convert_element_type.232) | copy-start | bytes 24580
  54.9 115.5 %copy-start.88 = (f32[512]{0:T(512)}, f32[512]{0:T(512)S(1)}, u32[]{:S(2)}) copy-start(f32[512]{0:T(512)S(1)} %fusion.174) | copy-start | bytes 6148
  78.0 103.7 %copy-start.65 = (f32[8,128]{1,0:T(8,128)}, f32[8,128]{1,0:T(8,128)S(1)}, u32[]{:S(2)}) copy-start(f32[8,128]{1,0:T(8,128)S(1)} %copy.105) | copy-start | bytes 12292
  78.1 103.6 %copy-start.73 = (f32[8,128]{1,0:T(8,128)}, f32[8,128]{1,0:T(8,128)S(1)}, u32[]{:S(2)}) copy-start(f32[8,128]{1,0:T(8,128)S(1)} %copy.104) | copy-start | bytes 12292
  78.2 103.6 %copy-start.79 = (f32[8,128]{1,0:T(8,128)}, f32[8,128]{1,0:T(8,128)S(1)}, u32[]{:S(2)}) copy-start(f32[8,128]{1,0:T(8,128)S(1)} %copy.103) | copy-start | bytes 12292
  78.3 111.1 %copy-start.69 = (f32[8,128]{1,0:T(8,128)}, f32[8,128]{1,0:T(8,128)S(1)}, u32[]{:S(2)}) copy-start(f32[8,128]{1,0:T(8,128)S(1)} %copy.113) | copy-start | bytes 12292
  78.4 111.1 %copy-start.77 = (f32[8,128]{1,0:T(8,128)}, f32[8,128]{1,0:T(8,128)S(1)}, u32[]{:S(2)}) copy-start(f32[8,128]{1,0:T(8,128)S(1)} %copy.112) | copy-start | bytes 12292
  78.5 111.0 %copy-start.83 = (f32[8,128]{1,0:T(8,128)}, f32[8,128]{1,0:T(8,128)S(1)}, u32[]{:S(2)}) copy-start(f32[8,128]{1,0:T(8,128)S(1)} %copy.111) | copy-start | bytes 12292
  78.5 110.9 %copy-start.71 = (f32[8,128]{1,0:T(8,128)}, f32[8,128]{1,0:T(8,128)S(1)}, u32[]{:S(2)}) copy-start(f32[8,128]{1,0:T(8,128)S(1)} %copy.110) | copy-start | bytes 12292
  78.6 110.9 %copy-start.75 = (f32[8,128]{1,0:T(8,128)}, f32[8,128]{1,0:T(8,128)S(1)}, u32[]{:S(2)}) copy-start(f32[8,128]{1,0:T(8,128)S(1)} %copy.109) | copy-start | bytes 12292
  78.7 110.8 %copy-start.81 = (f32[8,128]{1,0:T(8,128)}, f32[8,128]{1,0:T(8,128)S(1)}, u32[]{:S(2)}) copy-start(f32[8,128]{1,0:T(8,128)S(1)} %copy.108) | copy-start | bytes 12292
  78.8 110.7 %copy-start.85 = (f32[8,128]{1,0:T(8,128)}, f32[8,128]{1,0:T(8,128)S(1)}, u32[]{:S(2)}) copy-start(f32[8,128]{1,0:T(8,128)S(1)} %copy.107) | copy-start | bytes 12292
  78.8 110.7 %copy-start.67 = (f32[8,128]{1,0:T(8,128)}, f32[8,128]{1,0:T(8,128)S(1)}, u32[]{:S(2)}) copy-start(f32[8,128]{1,0:T(8,128)S(1)} %copy.106) | copy-start | bytes 12292
  111.9 545.2 %copy-start.109 = (f32[128]{0:T(128)}, f32[128]{0:T(128)S(1)}, u32[]{:S(2)}) copy-start(f32[128]{0:T(128)S(1)} %convert_element_type.207) | copy-start | bytes 1540
  112.5 1037.2 %copy-start.56 = (f32[512]{0:T(512)}, f32[512]{0:T(512)S(1)}, u32[]{:S(2)}) copy-start(f32[512]{0:T(512)S(1)} %get-tuple-element.705) | copy-start | bytes 6148
  112.5 1037.9 %copy-start.60 = (f32[512]{0:T(512)}, f32[512]{0:T(512)S(1)}, u32[]{:S(2)}) copy-start(f32[512]{0:T(512)S(1)} %get-tuple-element.707) | copy-start | bytes 6148
  112.5 1038.6 %copy-start.58 = (f32[512]{0:T(512)}, f32[512]{0:T(512)S(1)}, u32[]{:S(2)}) copy-start(f32[512]{0:T(512)S(1)} %get-tuple-element.706) | copy-start | bytes 6148
  665.1 1323.5 %all-gather.7.cloned.1.call-start = ((), (), s32[]{:S(2)}) async-start(), calls=%async_computation.5 | async-start | bytes 36765696 | tf_op jit(solution)/shard_map/all_gather | solution.py:215
  669.0 1440.0 %all-reduce.52.cloned.1.call-start = ((), (), s32[]{:S(2)}) async-start(), calls=%async_computation.6 | async-start | bytes 4194304 | tf_op jit(solution)/shard_map/psum | solution.py:237
  673.1 4.6 collective-permute-start
  684.6 95.7 %collective-permute-start.1 = (bf16[2,128,3,2816]{3,1,2,0:T(8,128)(2,1)}, bf16[2,128,3,2816]{3,1,2,0:T(8,128)(2,1)}, u32[]{:S(2)}, u32[]{:S(2)}) collective-permute-start(bf16[2,128,3,2816]{3,1,2,0:T(8,128)(2,1)} %pad_maximum_fusion.6), channel_id=1, source_target_pairs={{0,4},{2,6},{4,0},{6,2},{8,12},{10,14},{12,8},{14,10},{16,20},{18,... | collective-permute-start | bytes 12976136 | tf_op jit(solution)/shard_map/ppermute | solution.py:20
  794.7 335.0 %collective-permute-start.2 = (bf16[4,128,3,2816]{3,1,2,0:T(8,128)(2,1)}, bf16[4,128,3,2816]{3,1,2,0:T(8,128)(2,1)}, u32[]{:S(2)}, u32[]{:S(2)}) collective-permute-start(bf16[4,128,3,2816]{3,1,2,0:T(8,128)(2,1)} %pad_maximum_fusion.4), channel_id=1, source_target_pairs={{0,8},{2,10},{4,12},{6,14},{8,0},{10,2},{12,4},{14,6},{16,24},{18,... | collective-permute-start | bytes 25952264 | tf_op jit(solution)/shard_map/ppermute | solution.py:20
  1147.4 745.2 %collective-permute-start.3 = (bf16[8,128,3,2816]{3,1,2,0:T(8,128)(2,1)}, bf16[8,128,3,2816]{3,1,2,0:T(8,128)(2,1)}, u32[]{:S(2)}, u32[]{:S(2)}) collective-permute-start(bf16[8,128,3,2816]{3,1,2,0:T(8,128)(2,1)} %pad_maximum_fusion.3), channel_id=1, source_target_pairs={{0,16},{2,18},{4,20},{6,22},{8,24},{10,26},{12,28},{14,30},{16,0},... | collective-permute-start | bytes 51904520 | tf_op jit(solution)/shard_map/ppermute | solution.py:20
  1536.2 577.7 %copy-start.49 = (f32[16,1,128]{2,1,0:T(1,128)}, f32[16,1,128]{2,1,0:T(1,128)S(1)}, u32[]{:S(2)}) copy-start(f32[16,1,128]{2,1,0:T(1,128)S(1)} %convert_element_type.233) | copy-start | bytes 24580
  1968.1 145.9 %copy-start.90 = (f32[512]{0:T(512)}, f32[512]{0:T(512)S(1)}, u32[]{:S(2)}) copy-start(f32[512]{0:T(512)S(1)} %fusion.175) | copy-start | bytes 6148
  2022.3 826.8 %all-reduce.54.cloned.1.call-start = ((), (), s32[]{:S(2)}) async-start(), calls=%async_computation.10 | async-start | bytes 8388608 | tf_op jit(solution)/shard_map/psum | solution.py:206
  2128.6 541.0 %copy-start.40 = (f32[512,8]{0,1:T(8,128)S(1)}, f32[512,8]{0,1:T(8,128)}, u32[]{:S(2)}) copy-start(f32[512,8]{0,1:T(8,128)} %copy-done.39) | copy-start | bytes 49156
  2704.9 446.3 %reduce-scatter.5.cloned.1.call-start = ((), (), s32[]{:S(2)}) async-start(), calls=%async_computation.7 | async-start | bytes 35651584 | tf_op jit(solution)/shard_map/reduce_scatter | solution.py:256
  2750.3 456.1 %reduce-scatter.7.cloned.1.call-start = ((), (), s32[]{:S(2)}) async-start(), calls=%async_computation.8 | async-start | bytes 69632 | tf_op jit(solution)/shard_map/reduce_scatter | solution.py:278
  2793.1 1072.6 %reduce-scatter.9.cloned.1.call-start = ((), (), s32[]{:S(2)}) async-start(), calls=%async_computation.9 | async-start | bytes 73531392 | tf_op jit(solution)/shard_map/reduce_scatter | solution.py:228
  (112 other events, 808.1 us)
Sparse Core Ops, SparseCore 0:
  11.2 131.5 all-gather.4
  665.2 106.4 all-reduce.49
  773.4 319.1 all-gather.6
  2022.4 86.5 all-reduce.51
  2705.0 108.2 all-reduce.53
  2818.0 333.2 reduce-scatter.4
  3155.5 50.8 reduce-scatter.6
  3211.2 654.4 reduce-scatter.8
